TPU v7x, 32 devices: a whole 2x2x4 slice. The times are simulated.
32 devices in a mesh: seq: 2 (over core), narrow: 4 (over y, x), wide: 4 (over z).
Axes of the slice: x: 2, y: 2, z: 4, core: 2. Of those that a mesh axis runs over, the one named last changes fastest.
Arguments:
- tokens: bfloat16 [8192, 2048], P('seq', 'narrow'), may hold values from -6 to 6
- attn_gain: float32 [2048], P('narrow'), may hold values from 0.5 to 1.5
- w_query: bfloat16 [2048, 2048], P('narrow', 'wide'), may hold values from -0.125 to 0.125
- w_key: bfloat16 [2048, 512], P('narrow', 'wide'), may hold values from -0.125 to 0.125
- w_value: bfloat16 [2048, 512], P('narrow', 'wide'), may hold values from -0.125 to 0.125
- w_out: bfloat16 [2048, 2048], P('wide', 'narrow'), may hold values from -2 to 2
- ffn_gain: float32 [2048], P('narrow'), may hold values from 0.5 to 1.5
- w_gate: bfloat16 [2048, 8192], P('narrow', 'wide'), may hold values from -0.125 to 0.125
- w_up: bfloat16 [2048, 8192], P('narrow', 'wide'), may hold values from -0.125 to 0.125
- w_down: bfloat16 [8192, 2048], P('wide', 'narrow'), may hold values from -0.0625 to 0.0625
- segment_ids: int32 [8192], replicated, may hold values from 0 to 2, as said below
- token_mask: int32 [8192], replicated, may hold values from 0 to 1, as said below
- out_grad: bfloat16 [8192, 2048], P('seq', 'narrow'), may hold values from -6 to 6
Outputs:
- result: bfloat16 [8192, 2048], P('seq', 'narrow')
- input_grad: float32 [8192, 2048], P('seq', 'narrow')
- grad_attn_gain: float32 [2048], P('narrow')
- grad_w_query: float32 [2048, 2048], P('narrow', 'wide')
- grad_w_key: float32 [2048, 512], P('narrow', 'wide')
- grad_w_value: float32 [2048, 512], P('narrow', 'wide')
- grad_w_out: float32 [2048, 2048], P('wide', 'narrow')
- grad_ffn_gain: float32 [2048], P('narrow')
- grad_w_gate: float32 [2048, 8192], P('narrow', 'wide')
- grad_w_up: float32 [2048, 8192], P('narrow', 'wide')
- grad_w_down: float32 [8192, 2048], P('wide', 'narrow')
Inputs may be any that keep to these rules, and one draw needn't show every extreme that they name: `segment_ids`: the pack holds three sequences in order, ids 0, 1, 2, never falling: the first and the last hold 2 to 256 positions each, the middle one all the rest. `token_mask`: padding is the last positions of each sequence: 1 to 255 of the middle one; of the first and the last, one or more and fewer than the sequence's length; the first position of each sequence is a real token.
All inputs are finite; a program needn't handle non-finite values.
Results may differ from a plain program's by a relative error of at most 0.018.
Values may be sent and summed in bfloat16 or wider, within the bound.
A program may use at most 384 MiB of HBM per device.

v0:
```python
import jax
import jax.numpy as jnp
from jax import lax
from jax.sharding import PartitionSpec as P

D = 2048
HD = 64
EPS = 1e-05
THETA = 500000.0
NEG = -1e30


def positions(segment_ids):
    token_index = jnp.arange(segment_ids.shape[0], dtype=jnp.int32)
    seg_first = jnp.concatenate([jnp.ones((1,), dtype=bool), segment_ids[1:] != segment_ids[:-1]])
    seg_start = lax.cummax(jnp.where(seg_first, token_index, jnp.zeros_like(token_index)), axis=0)
    return token_index - seg_start


def rotation(token_pos):
    half_dim = HD // 2
    frequency = THETA ** (-2.0 * jnp.arange(half_dim, dtype=jnp.float32) / HD)
    angles = token_pos.astype(jnp.float32)[:, None] * frequency[None, :]
    cosine_table = jnp.concatenate([jnp.cos(angles), jnp.cos(angles)], axis=1)
    sine_table = jnp.concatenate([jnp.sin(angles), jnp.sin(angles)], axis=1)
    return (cosine_table, sine_table)


def rotate(vectors, cosine_table, sine_table, turn_sign):
    half_dim = HD // 2
    turned = jnp.concatenate([-vectors[..., half_dim:], vectors[..., :half_dim]], axis=-1)
    return vectors * cosine_table[:, None, :] + turn_sign * turned * sine_table[:, None, :]


def narrow_total(values):
    return lax.psum(values, "narrow")


def wide_total(values):
    return lax.psum(values, "wide")


def gather_rows(values):
    return lax.all_gather(values, "narrow", axis=0, tiled=True)


def rms_norm(values):
    squares = narrow_total(jnp.sum(values * values, axis=1))
    row_scale = lax.rsqrt(squares / D + EPS)
    return (values * row_scale[:, None], row_scale)


def norm_back(grad_h, normed, row_scale, gain_vec):
    grad_normed = grad_h * gain_vec[None, :]
    inner_sum = narrow_total(jnp.sum(grad_normed * normed, axis=1))
    grad_input = row_scale[:, None] * (grad_normed - normed * (inner_sum / D)[:, None])
    return (grad_input, jnp.sum(grad_h * normed, axis=0))


def sum_rows(left_side, weight, product_kind):

    def term_rows():
        if product_kind == "flip":
            return lax.dot_general(
                left_side, weight, (((1,), (1,)), ((), ())), preferred_element_type=jnp.float32
            )
        return jnp.dot(left_side, weight, preferred_element_type=jnp.float32)

    return lax.psum_scatter(term_rows(), "narrow", scatter_dimension=0, tiled=True)


def back_rows(grad_rows, weight, inputs):
    shard_piece = lax.all_gather(grad_rows, "narrow", axis=0, tiled=True)
    product = lax.dot_general(
        shard_piece, weight, (((1,), (1,)), ((), ())), preferred_element_type=jnp.float32
    )
    weight_grad = lax.dot_general(
        inputs, shard_piece, (((0,), (0,)), ((), ())), preferred_element_type=jnp.float32
    )
    return (product, weight_grad)


def body(
    tokens,
    attn_gain,
    w_query,
    w_key,
    w_value,
    w_out,
    ffn_gain,
    w_gate,
    w_up,
    w_down,
    segment_ids,
    token_mask,
    out_grad,
):
    narrow_count = lax.axis_size("narrow")
    tok_count = tokens.shape[0]
    quarter = tok_count // narrow_count
    total_tokens = segment_ids.shape[0]
    seq_index = lax.axis_index("seq")
    narrow_index = lax.axis_index("narrow")
    q_width = w_query.shape[1]
    kv_width = w_key.shape[1]
    q_heads = q_width // HD
    kv_heads = kv_width // HD
    group_size = q_heads // kv_heads
    ff_width = w_gate.shape[1]
    score_scale = HD ** (-0.5)
    cosine_all, sine_all = rotation(positions(segment_ids))
    own_first = seq_index * tok_count + narrow_index * quarter
    own_index = own_first + jnp.arange(quarter, dtype=jnp.int32)
    cosine_table = lax.dynamic_slice_in_dim(cosine_all, own_first, quarter, 0)
    sine_table = lax.dynamic_slice_in_dim(sine_all, own_first, quarter, 0)
    own_segment = lax.dynamic_slice_in_dim(segment_ids, own_first, quarter, 0)
    key_index = jnp.arange(total_tokens, dtype=jnp.int32)
    allowed = (
        (own_segment[:, None] == segment_ids[None, :])
        & (key_index[None, :] <= own_index[:, None])
        & (token_mask[None, :] == 1)
    )
    row_valid = lax.dynamic_slice_in_dim(token_mask, seq_index * tok_count, tok_count, 0)
    grad_low = jnp.where(row_valid[:, None] == 1, out_grad, jnp.zeros_like(out_grad))
    grad_float = grad_low.astype(jnp.float32)
    x_float = tokens.astype(jnp.float32)
    normed_one, scale_one = rms_norm(x_float)
    h_one = (normed_one * attn_gain[None, :]).astype(jnp.bfloat16)
    w_qkv = jnp.concatenate([w_query, w_key, w_value], axis=1)
    qkv_lin = sum_rows(h_one, w_qkv, "plain")
    query_rot = rotate(
        qkv_lin[:, :q_width].reshape(quarter, q_heads, HD), cosine_table, sine_table, 1.0
    ).astype(jnp.bfloat16)
    key_rot = rotate(
        qkv_lin[:, q_width : q_width + kv_width].reshape(quarter, kv_heads, HD),
        cosine_table,
        sine_table,
        1.0,
    ).astype(jnp.bfloat16)
    value_low = qkv_lin[:, q_width + kv_width :].astype(jnp.bfloat16)
    kv_local = jnp.concatenate([key_rot.reshape(quarter, kv_width), value_low], axis=1)
    kv_all = lax.all_gather(kv_local, ("seq", "narrow"), axis=0, tiled=True)
    keys_all = kv_all[:, :kv_width].reshape(total_tokens, kv_heads, HD)
    values_all = kv_all[:, kv_width:].reshape(total_tokens, kv_heads, HD)
    query_heads = jnp.transpose(query_rot, (1, 0, 2))
    head_ids = jnp.arange(q_heads, dtype=jnp.int32)

    def head_scores(query_one, head_id):
        kv_id = head_id // group_size
        key_one = lax.dynamic_index_in_dim(keys_all, kv_id, 1, keepdims=False)
        value_one = lax.dynamic_index_in_dim(values_all, kv_id, 1, keepdims=False)
        scores = (
            lax.dot_general(
                query_one, key_one, (((1,), (1,)), ((), ())), preferred_element_type=jnp.float32
            )
            * score_scale
        )
        return (jnp.where(allowed, scores, NEG), key_one, value_one)

    def head_forward(packed):
        query_one, head_id = packed
        scores, key_one, value_one = head_scores(query_one, head_id)
        row_top = jnp.max(scores, axis=1, keepdims=True)
        log_total = row_top + jnp.log(jnp.sum(jnp.exp(scores - row_top), axis=1, keepdims=True))
        prob_low = jnp.exp(scores - log_total).astype(jnp.bfloat16)
        return (jnp.dot(prob_low, value_one, preferred_element_type=jnp.float32), log_total[:, 0])

    head_out, log_totals = lax.map(head_forward, (query_heads, head_ids))
    attn_heads = jnp.transpose(head_out, (1, 0, 2)).reshape(quarter, q_width).astype(jnp.bfloat16)
    attn_all = gather_rows(attn_heads)
    middle = x_float + wide_total(jnp.dot(attn_all, w_out, preferred_element_type=jnp.float32))
    normed_two, scale_two = rms_norm(middle)
    h_two = (normed_two * ffn_gain[None, :]).astype(jnp.bfloat16)
    w_gate_up = jnp.concatenate([w_gate, w_up], axis=1)
    gate_up = sum_rows(h_two, w_gate_up, "plain")
    gate_lin = gate_up[:, :ff_width]
    up_lin = gate_up[:, ff_width:]
    gate_sig = jax.nn.sigmoid(gate_lin)
    act_low = (gate_lin * gate_sig * up_lin).astype(jnp.bfloat16)
    act_all = gather_rows(act_low)
    down_sum = wide_total(jnp.dot(act_all, w_down, preferred_element_type=jnp.float32))
    result = (middle + down_sum).astype(jnp.bfloat16)
    grad_w_down = lax.dot_general(
        act_all, grad_low, (((0,), (0,)), ((), ())), preferred_element_type=jnp.float32
    )
    act_grad = sum_rows(grad_low, w_down, "flip")
    gate_grad = act_grad * up_lin * gate_sig * (1.0 + gate_lin * (1.0 - gate_sig))
    up_grad = act_grad * gate_lin * gate_sig
    gate_up_grad = jnp.concatenate([gate_grad, up_grad], axis=1).astype(jnp.bfloat16)
    middle_part, grad_gate_up = back_rows(gate_up_grad, w_gate_up, h_two)
    middle_norm_grad, grad_ffn_gain = norm_back(
        wide_total(middle_part), normed_two, scale_two, ffn_gain
    )
    middle_grad = grad_float + middle_norm_grad
    attn_grad_low = middle_grad.astype(jnp.bfloat16)
    grad_w_out = lax.dot_general(
        attn_all, attn_grad_low, (((0,), (0,)), ((), ())), preferred_element_type=jnp.float32
    )
    heads_grad = sum_rows(attn_grad_low, w_out, "flip").astype(jnp.bfloat16)
    heads_grad_split = jnp.transpose(heads_grad.reshape(quarter, q_heads, HD), (1, 0, 2))

    def head_backward(packed):
        query_one, grad_one, log_total, head_id = packed
        scores, key_one, value_one = head_scores(query_one, head_id)
        attn_prob = jnp.exp(scores - log_total[:, None])
        prob_low = attn_prob.astype(jnp.bfloat16)
        prob_grad = lax.dot_general(
            grad_one, value_one, (((1,), (1,)), ((), ())), preferred_element_type=jnp.float32
        )
        inner_sum = jnp.sum(attn_prob * prob_grad, axis=1, keepdims=True)
        score_grad = (attn_prob * (prob_grad - inner_sum)).astype(jnp.bfloat16)
        query_grad = jnp.dot(score_grad, key_one, preferred_element_type=jnp.float32) * score_scale
        key_grad = (
            lax.dot_general(
                score_grad, query_one, (((0,), (0,)), ((), ())), preferred_element_type=jnp.float32
            )
            * score_scale
        )
        value_grad = lax.dot_general(
            prob_low, grad_one, (((0,), (0,)), ((), ())), preferred_element_type=jnp.float32
        )
        return (query_grad, key_grad, value_grad)

    query_grads, key_grads, value_grads = lax.map(
        head_backward, (query_heads, heads_grad_split, log_totals, head_ids)
    )
    key_sum = jnp.sum(key_grads.reshape(kv_heads, group_size, total_tokens, HD), axis=1)
    value_sum = jnp.sum(value_grads.reshape(kv_heads, group_size, total_tokens, HD), axis=1)
    kv_grad_all = jnp.concatenate(
        [
            jnp.transpose(key_sum, (1, 0, 2)).reshape(total_tokens, kv_width),
            jnp.transpose(value_sum, (1, 0, 2)).reshape(total_tokens, kv_width),
        ],
        axis=1,
    )
    kv_grad = lax.psum_scatter(
        kv_grad_all.astype(jnp.bfloat16), ("seq", "narrow"), scatter_dimension=0, tiled=True
    ).astype(jnp.float32)
    query_back = rotate(
        jnp.transpose(query_grads, (1, 0, 2)), cosine_table, sine_table, -1.0
    ).reshape(quarter, q_width)
    key_back = rotate(
        kv_grad[:, :kv_width].reshape(quarter, kv_heads, HD), cosine_table, sine_table, -1.0
    ).reshape(quarter, kv_width)
    qkv_grad = jnp.concatenate([query_back, key_back, kv_grad[:, kv_width:]], axis=1).astype(
        jnp.bfloat16
    )
    first_part, grad_qkv = back_rows(qkv_grad, w_qkv, h_one)
    input_part, grad_attn_gain = norm_back(wide_total(first_part), normed_one, scale_one, attn_gain)
    input_grad = middle_grad + input_part
    summed = (
        lax.psum(grad_attn_gain.astype(jnp.bfloat16), "seq").astype(jnp.float32),
        lax.psum(grad_qkv.astype(jnp.bfloat16), "seq").astype(jnp.float32),
        lax.psum(grad_w_out.astype(jnp.bfloat16), "seq").astype(jnp.float32),
        lax.psum(grad_ffn_gain.astype(jnp.bfloat16), "seq").astype(jnp.float32),
        lax.psum(grad_gate_up.astype(jnp.bfloat16), "seq").astype(jnp.float32),
        lax.psum(grad_w_down.astype(jnp.bfloat16), "seq").astype(jnp.float32),
    )
    qkv_total = summed[1]
    gate_up_total = summed[4]
    return (
        result,
        input_grad,
        summed[0],
        qkv_total[:, :q_width],
        qkv_total[:, q_width : q_width + kv_width],
        qkv_total[:, q_width + kv_width :],
        summed[2],
        summed[3],
        gate_up_total[:, :ff_width],
        gate_up_total[:, ff_width:],
        summed[5],
    )


def solution(mesh):
    return jax.shard_map(
        body,
        mesh=mesh,
        in_specs=(
            P("seq", "narrow"),
            P("narrow"),
            P("narrow", "wide"),
            P("narrow", "wide"),
            P("narrow", "wide"),
            P("wide", "narrow"),
            P("narrow"),
            P("narrow", "wide"),
            P("narrow", "wide"),
            P("wide", "narrow"),
            P(),
            P(),
            P("seq", "narrow"),
        ),
        out_specs=(
            P("seq", "narrow"),
            P("seq", "narrow"),
            P("narrow"),
            P("narrow", "wide"),
            P("narrow", "wide"),
            P("narrow", "wide"),
            P("wide", "narrow"),
            P("narrow"),
            P("narrow", "wide"),
            P("narrow", "wide"),
            P("wide", "narrow"),
        ),
        check_vma=False,
    )
```

profile of v0, /device:TPU:0, one launch (start us, length us, event | category | flops | bytes accessed | tf_op | source)
XLA Modules:
  0.0 4983.6 jit_solution(15209267365387991906)
XLA Ops:
  51.3 111.1 %reduce-scatter.5.cloned.1.call-done = f32[1024,768]{1,0:T(8,128)} async-done(((f32[4096,768]{1,0:T(8,128)}), f32[1024,768]{1,0:T(8,128)}) %reduce-scatter.5.cloned.1.call-update) | async-done | bytes 3145744 | tf_op jit(solution)/shard_map/reduce_scatter | solution.py:69
  217.7 410.5 %while.34 = (s32[]{:T(128)}, bf16[8,1024,64]{1,2,0:T(8,128)(2,1)S(1)}, f32[8,1024]{1,0:T(8,128)}, bf16[8,1024,64]{2,1,0:T(8,128)(2,1)}, s32[8]{0:T(128)S(1)}, /*...) while((s32[]{:T(128)}, ...), condition=%wide.region_8.9_spmd.clone.clone, body=%wide.region_5.8_spmd.clone.sunk.clone | while | flops 2239757312 | bytes 111760208 | solution.py:168
  629.6 52.4 %all-gather.8.cloned.1.call-done = bf16[4096,512]{0,1:T(8,128)(2,1)} async-done(((bf16[1024,512]{0,1:T(8,128)(2,1)}), bf16[4096,512]{0,1:T(8,128)(2,1)}) %all-gather.8.cloned.1.call-update) | async-done | bytes 4194320 | tf_op jit(solution)/shard_map/all_gather | solution.py:44
  714.4 266.7 %all-reduce.10.cloned.1.call-done = f32[4096,512]{1,0:T(8,128)} async-done(((f32[4096,512]{1,0:T(8,128)}), f32[4096,512]{1,0:T(8,128)}) %all-reduce.10.cloned.1.call-update) | async-done | bytes 8388624 | tf_op jit(solution)/shard_map/psum | solution.py:40
  1006.9 34.1 fusion.83
  1042.9 229.3 %reduce-scatter.7.cloned.1.call-done = f32[1024,2048]{1,0:T(8,128)} async-done(((f32[4096,2048]{1,0:T(8,128)}), f32[1024,2048]{1,0:T(8,128)}) %reduce-scatter.7.cloned.1.call-update) | async-done | bytes 8388624 | tf_op jit(solution)/shard_map/reduce_scatter | solution.py:69
  1272.2 1120.8 %all-reduce.14.cloned.1.call-done = f32[4096,4096]{1,0:T(8,128)} async-done(((f32[4096,4096]{1,0:T(8,128)}), f32[4096,4096]{1,0:T(8,128)}) %all-reduce.14.cloned.1.call-update) | async-done | bytes 67108880
  2415.0 298.5 %all-gather.12.cloned.1.call-done = bf16[4096,4096]{1,0:T(8,128)(2,1)} async-done(((bf16[1024,4096]{1,0:T(8,128)(2,1)}), bf16[4096,4096]{1,0:T(8,128)(2,1)}) %all-gather.12.cloned.1.call-update) | async-done | bytes 33554448 | tf_op jit(solution)/shard_map/all_gather | solution.py:73
  2738.6 290.9 %all-reduce.12.cloned.1.call-done = f32[4096,512]{1,0:T(8,128)} async-done(((f32[4096,512]{1,0:T(8,128)}), f32[4096,512]{1,0:T(8,128)}) %all-reduce.12.cloned.1.call-update) | async-done | bytes 8388624 | tf_op jit(solution)/shard_map/psum | solution.py:40
  3071.1 83.6 %reduce-scatter.9.cloned.1.call-done = f32[1024,512]{1,0:T(8,128)} async-done(((f32[4096,512]{1,0:T(8,128)}), f32[1024,512]{1,0:T(8,128)}) %reduce-scatter.9.cloned.1.call-update) | async-done | bytes 2097168 | tf_op jit(solution)/shard_map/reduce_scatter | solution.py:69
  3159.0 861.1 %while.35 = (s32[]{:T(128)}, f32[8,1024,64]{1,2,0:T(8,128)}, f32[8,8192,64]{1,2,0:T(8,128)}, f32[8,8192,64]{1,2,0:T(8,128)}, bf16[8,1024,64]{2,1,0:T(8,128)(2,1)...) while((s32[]{:T(128)}, f32[8,1024,64]{1,2,0:T(8,128)}, ...), condition=%wide.region_21.22_spmd.clone.clone, body=%wide.region_19.21_spmd.clone.sunk.clone | while | flops 5478349824 | bytes 344006528 | solution.py:224
  3178.0 28.8 multiply_reduce_fusion.6
  3206.8 27.5 multiply_convert_fusion.9
  3285.6 28.7 multiply_reduce_fusion.6
  3314.3 27.5 multiply_convert_fusion.9
  3393.1 28.7 multiply_reduce_fusion.6
  3421.8 27.5 multiply_convert_fusion.9
  3500.6 28.7 multiply_reduce_fusion.6
  3529.4 27.5 multiply_convert_fusion.9
  3608.2 28.7 multiply_reduce_fusion.6
  3637.0 27.5 multiply_convert_fusion.9
  3715.8 28.7 multiply_reduce_fusion.6
  3744.5 27.5 multiply_convert_fusion.9
  3823.3 28.7 multiply_reduce_fusion.6
  3852.1 27.5 multiply_convert_fusion.9
  3930.9 28.7 multiply_reduce_fusion.6
  3959.7 27.5 multiply_convert_fusion.9
  4039.5 46.7 reduce-scatter.11.cloned.1.call-done
  4090.9 155.2 %all-gather.10.cloned.1.call-done = bf16[4096,2048]{1,0:T(8,128)(2,1)} async-done(((bf16[1024,2048]{1,0:T(8,128)(2,1)}), bf16[4096,2048]{1,0:T(8,128)(2,1)}) %all-gather.10.cloned.1.call-update) | async-done | bytes 16777232 | tf_op jit(solution)/shard_map/all_gather | solution.py:44
  4261.0 25.4 convolution_convert_fusion
  4289.5 29.1 all-gather.14.cloned.1.call-done
  4375.6 554.8 %all-reduce.16.cloned.1.call-done = (f32[4096,512]{1,0:T(8,128)}, f32[4096,512]{1,0:T(8,128)}) async-done(((f32[4096,512]{1,0:T(8,128)}, f32[4096,512]{1,0:T(8,128)}), (f32[4096,512]{1,0:T(8,128)}, f32[4096,512]{1,0:T(8,128)})) %all-reduce.16.cloned.1.call-update) | async-done | bytes 16777232 | tf_op jit(solution)/shard_map/psum | solution.py:40
  (351 shorter events, 1176.9 us)
Async XLA Ops:
  7.2 683.1 %copy-start = (bf16[2048,512]{1,0:T(8,128)(2,1)S(1)}, bf16[2048,512]{1,0:T(8,128)(2,1)}, u32[]{:S(2)}) copy-start(bf16[2048,512]{1,0:T(8,128)(2,1)} %param.26) | copy-start | bytes 6291460
  7.2 155.2 %reduce-scatter.5.cloned.1.call-start = ((), (), s32[]{:S(2)}) async-start(), calls=%async_computation.4 | async-start | bytes 15728640 | tf_op jit(solution)/shard_map/reduce_scatter | solution.py:69
  42.1 162.9 %all-gather.6.cloned.1.call-start = ((), (), s32[]{:S(2)}) async-start(), calls=%async_computation.5 | async-start | bytes 4718592 | tf_op jit(solution)/shard_map/all_gather | solution.py:142
  43.7 124.9 %copy-start.21 = (s32[8192]{0:T(1024)S(1)}, s32[8192]{0:T(1024)}, u32[]{:S(2)}) copy-start(s32[8192]{0:T(1024)} %param.28) | copy-start | bytes 98308
  47.4 129.0 %copy-start.7 = (f32[1024,64]{0,1:T(8,128)}, f32[1024,64]{0,1:T(8,128)S(1)}, u32[]{:S(2)}) copy-start(f32[1024,64]{0,1:T(8,128)S(1)} %fusion.80) | copy-start | bytes 786436
  168.2 513.9 %all-gather.8.cloned.1.call-start = ((), (), s32[]{:S(2)}) async-start(), calls=%async_computation.6 | async-start | bytes 5242880 | tf_op jit(solution)/shard_map/all_gather | solution.py:44
  628.2 62.0 %copy-start.27 = (pred[8192]{0:T(1024)(128)(4,1)}, pred[8192]{0:T(1024)(128)(4,1)S(1)}, u32[]{:S(2)}) copy-start(pred[8192]{0:T(1024)(128)(4,1)S(1)} %get-tuple-element.864) | copy-start | bytes 24580
  628.2 62.0 %copy-start.31 = (s32[1024]{0:T(1024)}, s32[1024]{0:T(1024)S(1)}, u32[]{:S(2)}) copy-start(s32[1024]{0:T(1024)S(1)} %get-tuple-element.865) | copy-start | bytes 12292
  628.2 62.0 %copy-start.33 = (s32[1024]{0:T(1024)}, s32[1024]{0:T(1024)S(1)}, u32[]{:S(2)}) copy-start(s32[1024]{0:T(1024)S(1)} %get-tuple-element.866) | copy-start | bytes 12292
  629.1 61.1 %copy-start.22 = (s32[8192]{0:T(1024)S(1)}, s32[8192]{0:T(1024)}, u32[]{:S(2)}) copy-start(s32[8192]{0:T(1024)} %param.28) | copy-start | bytes 98308
  629.2 351.9 %all-reduce.10.cloned.1.call-start = ((), (), s32[]{:S(2)}) async-start(), calls=%async_computation.7 | async-start | bytes 16777216 | tf_op jit(solution)/shard_map/psum | solution.py:40
  690.2 582.0 %reduce-scatter.7.cloned.1.call-start = ((), (), s32[]{:S(2)}) async-start(), calls=%async_computation.9 | async-start | bytes 41943040 | tf_op jit(solution)/shard_map/reduce_scatter | solution.py:69
  690.2 2362.8 %copy-start.23 = (pred[4096]{0:T(1024)(128)(4,1)}, pred[4096]{0:T(1024)(128)(4,1)S(1)}, u32[]{:S(2)}) copy-start(pred[4096]{0:T(1024)(128)(4,1)S(1)} %dynamic-slice_compare_fusion) | copy-start | bytes 12292
  708.0 1684.9 %all-reduce.14.cloned.1.call-start = ((), (), s32[]{:S(2)}) async-start(), calls=%async_computation.15 | async-start | bytes 134217728
  714.4 292.4 %copy-start.25 = (f32[512]{0:T(512)S(1)}, f32[512]{0:T(512)}, u32[]{:S(2)}) copy-start(f32[512]{0:T(512)} %param.23) | copy-start | bytes 6148
  1006.9 2046.2 %copy-start.19 = (f32[4096]{0:T(1024)}, f32[4096]{0:T(1024)S(1)}, u32[]{:S(2)}) copy-start(f32[4096]{0:T(1024)S(1)} %add_rsqrt_fusion) | copy-start | bytes 49156
  1041.0 1672.5 %all-gather.12.cloned.1.call-start = ((), (), s32[]{:S(2)}) async-start(), calls=%async_computation.10 | async-start | bytes 41943040 | tf_op jit(solution)/shard_map/all_gather | solution.py:73
  2414.8 614.8 %all-reduce.12.cloned.1.call-start = ((), (), s32[]{:S(2)}) async-start(), calls=%async_computation.11 | async-start | bytes 16777216 | tf_op jit(solution)/shard_map/psum | solution.py:40
  2738.6 416.2 %reduce-scatter.9.cloned.1.call-start = ((), (), s32[]{:S(2)}) async-start(), calls=%async_computation.12 | async-start | bytes 10485760 | tf_op jit(solution)/shard_map/reduce_scatter | solution.py:69
  3071.0 88.0 %copy-start.16 = (s32[8192]{0:T(1024)S(1)}, s32[8192]{0:T(1024)}, u32[]{:S(2)}) copy-start(s32[8192]{0:T(1024)} %param.27) | copy-start | bytes 98308
  3071.0 88.0 %copy-start.28 = (pred[8192]{0:T(1024)(128)(4,1)S(1)}, pred[8192]{0:T(1024)(128)(4,1)}, u32[]{:S(2)}) copy-start(pred[8192]{0:T(1024)(128)(4,1)} %copy-done.27) | copy-start | bytes 24580
  3071.0 88.0 %copy-start.32 = (s32[1024]{0:T(1024)S(1)}, s32[1024]{0:T(1024)}, u32[]{:S(2)}) copy-start(s32[1024]{0:T(1024)} %copy-done.31) | copy-start | bytes 12292
  3071.0 88.0 %copy-start.34 = (s32[1024]{0:T(1024)S(1)}, s32[1024]{0:T(1024)}, u32[]{:S(2)}) copy-start(s32[1024]{0:T(1024)} %copy-done.33) | copy-start | bytes 12292
  3071.0 1015.2 %reduce-scatter.11.cloned.1.call-start = ((), (), s32[]{:S(2)}) async-start(), calls=%async_computation.13 | async-start | bytes 4718592 | tf_op jit(solution)/shard_map/reduce_scatter | solution.py:236
  4034.8 211.3 %all-gather.10.cloned.1.call-start = ((), (), s32[]{:S(2)}) async-start(), calls=%async_computation.8 | async-start | bytes 20971520 | tf_op jit(solution)/shard_map/all_gather | solution.py:44
  4035.5 283.1 %all-gather.14.cloned.1.call-start = ((), (), s32[]{:S(2)}) async-start(), calls=%async_computation.14 | async-start | bytes 7864320 | tf_op jit(solution)/shard_map/all_gather | solution.py:73
  4037.3 208.8 %copy-start.24 = (pred[4096]{0:T(1024)(128)(4,1)S(1)}, pred[4096]{0:T(1024)(128)(4,1)}, u32[]{:S(2)}) copy-start(pred[4096]{0:T(1024)(128)(4,1)} %copy-done.23) | copy-start | bytes 12292
  4090.8 170.2 %copy-start.20 = (f32[4096]{0:T(1024)S(1)}, f32[4096]{0:T(1024)}, u32[]{:S(2)}) copy-start(f32[4096]{0:T(1024)} %copy-done.19) | copy-start | bytes 49156
  4090.8 170.2 %copy-start.26 = (f32[512]{0:T(512)S(1)}, f32[512]{0:T(512)}, u32[]{:S(2)}) copy-start(f32[512]{0:T(512)} %param.23) | copy-start | bytes 6148
  4090.8 271.9 %all-reduce.18.cloned.1.call-start = ((), (), s32[]{:S(2)}) async-start(), calls=%async_computation.17 | async-start | bytes 15204352 | tf_op jit(solution)/shard_map/psum | solution.py:253
  4327.7 602.7 %all-reduce.16.cloned.1.call-start = ((), (), s32[]{:S(2)}) async-start(), calls=%async_computation.16 | async-start | bytes 33554432 | tf_op jit(solution)/shard_map/psum | solution.py:40
  4375.6 560.7 %copy-start.30 = (bf16[512]{0:T(512)(128)(2,1)S(1)}, bf16[512]{0:T(512)(128)(2,1)}, u32[]{:S(2)}) copy-start(bf16[512]{0:T(512)(128)(2,1)} %get-tuple-element.396) | copy-start | bytes 3076
  (48 other events, 629.2 us)
Sparse Core Ops, SparseCore 0:
  42.2 120.1 reduce-scatter.4
  168.3 36.6 all-gather.5
  629.3 52.7 all-gather.7
  690.2 290.8 all-reduce.9
  984.0 288.1 reduce-scatter.6
  1275.9 1116.9 all-reduce.13
  2414.9 298.5 all-gather.11
  2738.7 290.8 all-reduce.11
  3071.1 83.5 reduce-scatter.8
  4034.9 51.2 reduce-scatter.10
  4088.7 157.4 all-gather.9
  4248.4 70.1 all-gather.13
  4327.8 34.8 all-reduce.17
  4366.0 564.4 all-reduce.15
where the time goes:
time: 4990 us; the launch traced here: 4980 us
  waiting for transfers between devices  3270 us (66%)
  matrix products  1040 us (21%)
  other arithmetic  454 us (9%)
  local copies, waits for them, and re-layouts  90.9 us (2%)
  blocking collectives  68.5 us (1%)
    unnamed x15, waiting for transfers between devices  1120 us
    psum x3, waiting for transfers between devices, wide_total(): return lax.psum(values, 'wide')  1110 us
    reduce_scatter x3, waiting for transfers between devices, sum_rows(): lax.psum_scatter(term_rows(), 'narrow', scatter_dimension=0, tiled=True)  424 us
    dot_general x16, matrix products, head_scores(): lax.dot_general(query_one, key_one, (((1,), (1,)), ((), ())), preferred_e...  386 us
    all_gather x2, waiting for transfers between devices, back_rows(): shard_piece = lax.all_gather(grad_rows, 'narrow', axis=0, tiled=True)  328 us
    convert_element_type x8, other arithmetic, head_backward(): score_grad = (attn_prob * (prob_grad - inner_sum)).astype(jnp.bfloat16)  220 us
    all_gather x2, waiting for transfers between devices, gather_rows(): return lax.all_gather(values, 'narrow', axis=0, tiled=True)  208 us
    dot_general x8, matrix products, head_backward(): lax.dot_general(prob_low, grad_one, (((0,), (0,)), ((), ())), preferred_e...  119 us
  transfers between devices with their start and end apart: 14, of which 14 were waited for; matrix products, arithmetic and copies ran while one was open for 4% of the time, Pallas kernels for 0%

commit v1 on v0

--- a/solution.py
+++ b/solution.py
@@ -2,6 +2,7 @@
 import jax.numpy as jnp
 from jax import lax
 from jax.sharding import PartitionSpec as P
+from jax.lax import all_gather
 
 D = 2048
 HD = 64
@@ -37,7 +38,12 @@
 
 
 def wide_total(values):
-    return lax.psum(values, "wide")
+
+    def balance_column(state):
+        right_arr = jnp.sum(all_gather(state, "wide"), axis=0)
+        return right_arr
+
+    return balance_column(values)
 
 
 def gather_rows(values):

time: 4990 us -> 6080 us (1.22)
  waiting for transfers between devices: 3270 us -> 4290 us
  other arithmetic: 454 us -> 520 us
    all_gather x0 -> x4, waiting for transfers between devices: none -> 2160 us  [balance_column(): right_arr = jnp.sum(all_gather(state, 'wide'), axis=0)]
    psum x3 -> x0, waiting for transfers between devices: 1110 us -> none  [wide_total(): return lax.psum(values, 'wide')]
    reduce_sum x0 -> x4, other arithmetic: none -> 71.7 us  [balance_column(): right_arr = jnp.sum(all_gather(state, 'wide'), axis=0)]
    unnamed x15 -> x16, waiting for transfers between devices: 1120 us -> 1120 us
  transfers between devices with their start and end apart: 14 -> 15, of which waited for: 14 -> 15; matrix products, arithmetic and copies ran while one was open for 4% -> 4% of each run, Pallas kernels for 0% -> 0%
where the time goes in v1:
time: 6080 us; the launch traced here: 6070 us
  waiting for transfers between devices  4290 us (71%)
  matrix products  1030 us (17%)
  other arithmetic  520 us (9%)
  local copies, waits for them, and re-layouts  94.2 us (2%)
  blocking collectives  68.8 us (1%)
    all_gather x4, waiting for transfers between devices, balance_column(): right_arr = jnp.sum(all_gather(state, 'wide'), axis=0)  2160 us
    unnamed x16, waiting for transfers between devices  1120 us
    reduce_scatter x3, waiting for transfers between devices, sum_rows(): lax.psum_scatter(term_rows(), 'narrow', scatter_dimension=0, tiled=True)  404 us
    dot_general x16, matrix products, head_scores(): lax.dot_general(query_one, key_one, (((1,), (1,)), ((), ())), preferred_e...  387 us
    all_gather x2, waiting for transfers between devices, back_rows(): shard_piece = lax.all_gather(grad_rows, 'narrow', axis=0, tiled=True)  310 us
    convert_element_type x8, other arithmetic, head_backward(): score_grad = (attn_prob * (prob_grad - inner_sum)).astype(jnp.bfloat16)  220 us
    all_gather x2, waiting for transfers between devices, gather_rows(): return lax.all_gather(values, 'narrow', axis=0, tiled=True)  203 us
  transfers between devices with their start and end apart: 15, of which 15 were waited for; matrix products, arithmetic and copies ran while one was open for 4% of the time, Pallas kernels for 0%

profile of v1, /device:TPU:0, one launch (start us, length us, event | category | flops | bytes accessed | tf_op | source)
XLA Modules:
  0.0 6068.2 jit_solution(7312360640050126742)
XLA Ops:
  51.3 111.1 %reduce-scatter.5.cloned.1.call-done = f32[1024,768]{1,0:T(8,128)} async-done(((f32[4096,768]{1,0:T(8,128)}), f32[1024,768]{1,0:T(8,128)}) %reduce-scatter.5.cloned.1.call-update) | async-done | bytes 3145744 | tf_op jit(solution)/shard_map/reduce_scatter | solution.py:75
  217.7 410.7 %while.34 = (s32[]{:T(128)}, bf16[8,1024,64]{1,2,0:T(8,128)(2,1)S(1)}, f32[8,1024]{1,0:T(8,128)}, bf16[8,1024,64]{2,1,0:T(8,128)(2,1)}, s32[8]{0:T(128)S(1)}, /*...) while((s32[]{:T(128)}, ...), condition=%wide.region_8.9_spmd.clone.clone, body=%wide.region_5.8_spmd.clone.sunk.clone | while | flops 2239757312 | bytes 111760208 | solution.py:174
  629.5 52.6 all-gather.16.cloned.1.call-done
  721.2 530.6 %all-gather.24.cloned.1.call-done = f32[16384,512]{1,0:T(8,128)} async-done(((f32[4096,512]{1,0:T(8,128)}), f32[16384,512]{1,0:T(8,128)}) %all-gather.24.cloned.1.call-update) | async-done | bytes 33554448 | tf_op jit(solution)/shard_map/all_gather | solution.py:43
  1295.4 34.2 fusion.83
  1331.6 210.5 %reduce-scatter.7.cloned.1.call-done = f32[1024,2048]{1,0:T(8,128)} async-done(((f32[4096,2048]{1,0:T(8,128)}), f32[1024,2048]{1,0:T(8,128)}) %reduce-scatter.7.cloned.1.call-update) | async-done | bytes 8388624 | tf_op jit(solution)/shard_map/reduce_scatter | solution.py:75
  1542.1 1120.8 %all-reduce.6.cloned.1.call-done = f32[4096,4096]{1,0:T(8,128)} async-done(((f32[4096,4096]{1,0:T(8,128)}), f32[4096,4096]{1,0:T(8,128)}) %all-reduce.6.cloned.1.call-update) | async-done | bytes 67108880
  2685.2 150.5 %all-gather.18.cloned.1.call-done = bf16[4096,2048]{1,0:T(8,128)(2,1)} async-done(((bf16[1024,2048]{1,0:T(8,128)(2,1)}), bf16[4096,2048]{1,0:T(8,128)(2,1)}) %all-gather.18.cloned.1.call-update) | async-done | bytes 16777232 | tf_op jit(solution)/shard_map/all_gather | solution.py:50
  2850.9 283.8 %all-gather.20.cloned.1.call-done = bf16[4096,4096]{1,0:T(8,128)(2,1)} async-done(((bf16[1024,4096]{1,0:T(8,128)(2,1)}), bf16[4096,4096]{1,0:T(8,128)(2,1)}) %all-gather.20.cloned.1.call-update) | async-done | bytes 33554448 | tf_op jit(solution)/shard_map/all_gather | solution.py:79
  3134.7 27.1 fusion.91
  3161.9 535.8 %all-gather.26.cloned.1.call-done = f32[16384,512]{1,0:T(8,128)} async-done(((f32[4096,512]{1,0:T(8,128)}), f32[16384,512]{1,0:T(8,128)}) %all-gather.26.cloned.1.call-update) | async-done | bytes 33554448 | tf_op jit(solution)/shard_map/all_gather | solution.py:43
  3718.4 540.4 %all-gather.28.cloned.1.call-done = f32[16384,512]{1,0:T(8,128)} async-done(((f32[4096,512]{1,0:T(8,128)}), f32[16384,512]{1,0:T(8,128)}) %all-gather.28.cloned.1.call-update) | async-done | bytes 33554448 | tf_op jit(solution)/shard_map/all_gather | solution.py:43
  4320.6 82.9 %reduce-scatter.9.cloned.1.call-done = f32[1024,512]{1,0:T(8,128)} async-done(((f32[4096,512]{1,0:T(8,128)}), f32[1024,512]{1,0:T(8,128)}) %reduce-scatter.9.cloned.1.call-update) | async-done | bytes 2097168 | tf_op jit(solution)/shard_map/reduce_scatter | solution.py:75
  4407.7 849.8 %while.35 = (s32[]{:T(128)}, f32[8,1024,64]{1,2,0:T(8,128)}, f32[8,8192,64]{1,2,0:T(8,128)}, f32[8,8192,64]{1,2,0:T(8,128)}, bf16[8,1024,64]{2,1,0:T(8,128)(2,1)...) while((s32[]{:T(128)}, f32[8,1024,64]{1,2,0:T(8,128)}, ...), condition=%wide.region_21.22_spmd.clone.clone, body=%wide.region_19.21_spmd.clone.sunk.clone | while | flops 5478349824 | bytes 344006080 | solution.py:230
  4425.1 28.7 multiply_reduce_fusion.6
  4453.8 27.5 multiply_convert_fusion.9
  4531.2 28.7 multiply_reduce_fusion.6
  4560.0 27.5 multiply_convert_fusion.9
  4637.3 28.7 multiply_reduce_fusion.6
  4666.1 27.5 multiply_convert_fusion.9
  4743.5 28.7 multiply_reduce_fusion.6
  4772.2 27.5 multiply_convert_fusion.9
  4849.7 28.7 multiply_reduce_fusion.6
  4878.4 27.5 multiply_convert_fusion.9
  4955.9 28.7 multiply_reduce_fusion.6
  4984.6 27.5 multiply_convert_fusion.9
  5062.0 28.7 multiply_reduce_fusion.6
  5090.8 27.5 multiply_convert_fusion.9
  5168.1 28.7 multiply_reduce_fusion.6
  5196.9 27.5 multiply_convert_fusion.9
  5276.0 47.7 reduce-scatter.11.cloned.1.call-done
  5457.6 549.8 %all-gather.30.cloned.1.call-done = f32[16384,512]{1,0:T(8,128)} async-done(((f32[4096,512]{1,0:T(8,128)}), f32[16384,512]{1,0:T(8,128)}) %all-gather.30.cloned.1.call-update) | async-done | bytes 33554448 | tf_op jit(solution)/shard_map/all_gather | solution.py:43
  (365 shorter events, 1282.5 us)
Async XLA Ops:
  7.2 683.8 %copy-start = (bf16[2048,512]{1,0:T(8,128)(2,1)S(1)}, bf16[2048,512]{1,0:T(8,128)(2,1)}, u32[]{:S(2)}) copy-start(bf16[2048,512]{1,0:T(8,128)(2,1)} %param.26) | copy-start | bytes 6291460
  7.2 155.2 %reduce-scatter.5.cloned.1.call-start = ((), (), s32[]{:S(2)}) async-start(), calls=%async_computation.4 | async-start | bytes 15728640 | tf_op jit(solution)/shard_map/reduce_scatter | solution.py:75
  42.1 162.9 %all-gather.14.cloned.1.call-start = ((), (), s32[]{:S(2)}) async-start(), calls=%async_computation.5 | async-start | bytes 4718592 | tf_op jit(solution)/shard_map/all_gather | solution.py:148
  43.7 125.2 %copy-start.24 = (s32[8192]{0:T(1024)S(1)}, s32[8192]{0:T(1024)}, u32[]{:S(2)}) copy-start(s32[8192]{0:T(1024)} %param.28) | copy-start | bytes 98308
  47.4 129.3 %copy-start.10 = (f32[1024,64]{0,1:T(8,128)}, f32[1024,64]{0,1:T(8,128)S(1)}, u32[]{:S(2)}) copy-start(f32[1024,64]{0,1:T(8,128)S(1)} %fusion.80) | copy-start | bytes 786436
  168.1 514.0 %all-gather.16.cloned.1.call-start = ((), (), s32[]{:S(2)}) async-start(), calls=%async_computation.6 | async-start | bytes 5242880 | tf_op jit(solution)/shard_map/all_gather | solution.py:50
  628.3 62.0 %copy-start.31 = (pred[8192]{0:T(1024)(128)(4,1)}, pred[8192]{0:T(1024)(128)(4,1)S(1)}, u32[]{:S(2)}) copy-start(pred[8192]{0:T(1024)(128)(4,1)S(1)} %get-tuple-element.862) | copy-start | bytes 24580
  628.3 62.0 %copy-start.35 = (s32[1024]{0:T(1024)}, s32[1024]{0:T(1024)S(1)}, u32[]{:S(2)}) copy-start(s32[1024]{0:T(1024)S(1)} %get-tuple-element.863) | copy-start | bytes 12292
  628.3 62.0 %copy-start.37 = (s32[1024]{0:T(1024)}, s32[1024]{0:T(1024)S(1)}, u32[]{:S(2)}) copy-start(s32[1024]{0:T(1024)S(1)} %get-tuple-element.864) | copy-start | bytes 12292
  629.3 61.0 %copy-start.25 = (s32[8192]{0:T(1024)S(1)}, s32[8192]{0:T(1024)}, u32[]{:S(2)}) copy-start(s32[8192]{0:T(1024)} %param.28) | copy-start | bytes 98308
  629.3 622.5 %all-gather.24.cloned.1.call-start = ((), (), s32[]{:S(2)}) async-start(), calls=%async_computation.13 | async-start | bytes 41943040 | tf_op jit(solution)/shard_map/all_gather | solution.py:43
  690.3 851.8 %reduce-scatter.7.cloned.1.call-start = ((), (), s32[]{:S(2)}) async-start(), calls=%async_computation.8 | async-start | bytes 41943040 | tf_op jit(solution)/shard_map/reduce_scatter | solution.py:75
  714.5 1948.4 %all-reduce.6.cloned.1.call-start = ((), (), s32[]{:S(2)}) async-start(), calls=%async_computation.17 | async-start | bytes 134217728
  1295.4 3003.6 %copy-start.22 = (f32[4096]{0:T(1024)}, f32[4096]{0:T(1024)S(1)}, u32[]{:S(2)}) copy-start(f32[4096]{0:T(1024)S(1)} %add_rsqrt_fusion) | copy-start | bytes 49156
  1329.7 1505.9 %all-gather.18.cloned.1.call-start = ((), (), s32[]{:S(2)}) async-start(), calls=%async_computation.7 | async-start | bytes 20971520 | tf_op jit(solution)/shard_map/all_gather | solution.py:50
  2676.7 458.1 %all-gather.20.cloned.1.call-start = ((), (), s32[]{:S(2)}) async-start(), calls=%async_computation.9 | async-start | bytes 41943040 | tf_op jit(solution)/shard_map/all_gather | solution.py:79
  2684.6 1013.1 %all-gather.26.cloned.1.call-start = ((), (), s32[]{:S(2)}) async-start(), calls=%async_computation.14 | async-start | bytes 41943040 | tf_op jit(solution)/shard_map/all_gather | solution.py:43
  2850.8 1408.0 %all-gather.28.cloned.1.call-start = ((), (), s32[]{:S(2)}) async-start(), calls=%async_computation.15 | async-start | bytes 41943040 | tf_op jit(solution)/shard_map/all_gather | solution.py:43
  3161.9 1241.6 %reduce-scatter.9.cloned.1.call-start = ((), (), s32[]{:S(2)}) async-start(), calls=%async_computation.10 | async-start | bytes 10485760 | tf_op jit(solution)/shard_map/reduce_scatter | solution.py:75
  4320.5 87.2 %copy-start.5 = (bf16[8192,2,64]{0,2,1:T(8,128)(2,1)S(1)}, bf16[8192,2,64]{0,2,1:T(8,128)(2,1)}, u32[]{:S(2)}) copy-start(bf16[8192,2,64]{0,2,1:T(8,128)(2,1)} %get-tuple-element.812) | copy-start | bytes 6291460
  4320.5 87.2 %copy-start.19 = (s32[8192]{0:T(1024)S(1)}, s32[8192]{0:T(1024)}, u32[]{:S(2)}) copy-start(s32[8192]{0:T(1024)} %param.27) | copy-start | bytes 98308
  4320.5 87.2 %copy-start.32 = (pred[8192]{0:T(1024)(128)(4,1)S(1)}, pred[8192]{0:T(1024)(128)(4,1)}, u32[]{:S(2)}) copy-start(pred[8192]{0:T(1024)(128)(4,1)} %copy-done.31) | copy-start | bytes 24580
  4320.5 87.2 %copy-start.36 = (s32[1024]{0:T(1024)S(1)}, s32[1024]{0:T(1024)}, u32[]{:S(2)}) copy-start(s32[1024]{0:T(1024)} %copy-done.35) | copy-start | bytes 12292
  4320.5 87.2 %copy-start.38 = (s32[1024]{0:T(1024)S(1)}, s32[1024]{0:T(1024)}, u32[]{:S(2)}) copy-start(s32[1024]{0:T(1024)} %copy-done.37) | copy-start | bytes 12292
  4320.5 1003.3 %reduce-scatter.11.cloned.1.call-start = ((), (), s32[]{:S(2)}) async-start(), calls=%async_computation.11 | async-start | bytes 4718592 | tf_op jit(solution)/shard_map/reduce_scatter | solution.py:242
  5272.3 126.3 %all-gather.22.cloned.1.call-start = ((), (), s32[]{:S(2)}) async-start(), calls=%async_computation.12 | async-start | bytes 7864320 | tf_op jit(solution)/shard_map/all_gather | solution.py:79
  5274.2 54.2 copy-start.28
  5328.3 114.4 %all-reduce.8.cloned.1.call-start = ((), (), s32[]{:S(2)}) async-start(), calls=%async_computation.18 | async-start | bytes 15204352 | tf_op jit(solution)/shard_map/psum | solution.py:259
  5328.4 40.4 slice-start
  5368.8 29.8 copy-start.21
  5372.0 35.8 copy-start.17
  5407.7 599.7 %all-gather.30.cloned.1.call-start = ((), (), s32[]{:S(2)}) async-start(), calls=%async_computation.16 | async-start | bytes 41943040 | tf_op jit(solution)/shard_map/all_gather | solution.py:43
  (53 other events, 634.1 us)
Sparse Core Ops, SparseCore 0:
  42.2 120.1 reduce-scatter.4
  168.3 36.6 all-gather.13
  629.4 52.6 all-gather.15
  690.4 561.3 all-gather.23
  1254.7 287.2 reduce-scatter.6
  1545.8 1116.9 all-reduce.5
  2676.8 158.8 all-gather.17
  2837.5 297.2 all-gather.19
  3136.3 561.3 all-gather.25
  3699.2 559.5 all-gather.27
  4320.7 82.7 reduce-scatter.8
  5272.5 51.2 reduce-scatter.10
  5328.4 70.1 all-gather.21
  5407.8 34.8 all-reduce.7
  5444.8 562.5 all-gather.29
